TPU v7x, 32 devices: a whole 2x2x4 slice. The times are simulated.
32 devices in a mesh: group: 4 (over x, core), tensor: 8 (over z, y).
Axes of the slice: x: 2, y: 2, z: 4, core: 2. Of those that a mesh axis runs over, the one named last changes fastest.
Arguments:
- hidden: bfloat16 [512, 8192], P('group'), may hold values from -6 to 6
- norm_gain: bfloat16 [8192], replicated, may hold values from 0.5 to 1.5
- query_matrix: bfloat16 [8192, 8192], P(None, 'tensor'), may hold values from -0.0625 to 0.0625
- output_weight: bfloat16 [8192, 8192], P('tensor'), may hold values from -0.0625 to 0.0625
- kv_pages: bfloat16 [768, 8, 32, 256], P('group', 'tensor'), may hold values from -400 to 400
- page_order: int32 [4, 192], P('group'), may hold values from 0 to 191, each once within a row
- page_counts: int32 [4, 128], P('group'), may hold values from 1 to 8, 192 in all within a row
- page_trims: int32 [4, 128], P('group'), may hold values from 0 to 31
- adapter_store: bfloat16 [32, 8192, 256], P('group', 'tensor'), may hold values from -0.0625 to 0.0625
- store_route: int32 [32, 1], replicated, may hold values from 0 to 3; in each aligned block of 8 rows (0 to 7, 8 to 15, ...) at most 4 rows name the same one
- store_slot: int32 [32], replicated, may hold values from 0 to 7
Outputs:
- layer_out: bfloat16 [512, 8192], P('group')
Inputs may be any that keep to these rules, and one draw needn't show every extreme that they name: `store_route`: in each group's block of 8 segments no store group is named more than 4 times. `page_order`: each group's row names each of its 192 pages once. `page_counts`: each group's counts sum to 192.
All inputs are finite; a program needn't handle non-finite values.
Results may differ from a plain program's by a relative error of at most 0.0092.
Values may be sent and summed in bfloat16 or wider, within the bound.
No kernel may reach another device: no remote copies, remote signals or barrier semaphores. Data moves between devices by JAX's collectives and lax.ppermute only.
A program may use at most 128 MiB of HBM per device.

v0:
```python
import math
import jax
import jax.numpy as jnp
from jax import lax
from jax.sharding import PartitionSpec as P

KVH = 8
HD = 128
SEG = 16
PAGES_MAX = 8
adapter_scale = 2.0
norm_eps = 1e-05
rope_base = 500000.0


def partner_2(value, axis, stride):
    return lax.ppermute(value, axis, [(i, i ^ 1 << stride) for i in range(lax.axis_size(axis))])


def rotate(queries, positions):
    half_dim = queries.shape[-1] // 2
    frequency = rope_base ** (-(jnp.arange(half_dim).astype(jnp.float32) * 2.0) / queries.shape[-1])
    angles = positions[:, None] * frequency[None, :]
    cosine = jnp.cos(angles)[:, None, :]
    sine_table = jnp.sin(angles)[:, None, :]
    lower_part = queries[..., :half_dim]
    upper_part = queries[..., half_dim:]
    return jnp.concatenate(
        [
            lower_part * cosine - upper_part * sine_table,
            upper_part * cosine + lower_part * sine_table,
        ],
        axis=-1,
    )


def rank_total(partial_value):
    return lax.psum(partial_value, "tensor")


def body(
    hidden,
    norm_gain,
    query_matrix,
    output_weight,
    kv_pages,
    page_order,
    page_counts,
    page_trims,
    adapter_store,
    store_route,
    store_slot,
):
    tensor_size = lax.axis_size("tensor")
    group_size = lax.axis_size("group")
    shard_tensor_index = lax.axis_index("tensor")
    group_index = lax.axis_index("group")
    row_count = hidden.shape[0]
    local_width = query_matrix.shape[1]
    heads_dev = local_width // HD
    split_count = tensor_size // KVH
    part_index = shard_tensor_index % split_count
    pool_size = kv_pages.shape[0]
    half_size = kv_pages.shape[2]
    stored = adapter_store.shape[0]
    lane_count = adapter_store.shape[2]
    adapter_rank_width = lane_count // 4
    seg_count = row_count // SEG
    capacity = max(2, (2 * seg_count + group_size - 1) // group_size)
    hidden_float32 = hidden.astype(jnp.float32)
    inv_rms = lax.rsqrt(jnp.mean(hidden_float32 * hidden_float32, axis=1, keepdims=True) + norm_eps)
    normalized_hidden = (hidden_float32 * inv_rms * norm_gain.astype(jnp.float32)[None, :]).astype(
        jnp.bfloat16
    )
    normalized_local = lax.dynamic_slice_in_dim(
        normalized_hidden, shard_tensor_index * local_width, local_width, 1
    )
    route_table = store_route[:, 0].reshape(group_size, seg_count)
    slot_table = store_slot.reshape(group_size, seg_count)
    earlier = jnp.arange(seg_count)[:, None] > jnp.arange(seg_count)[None, :]
    same_route = route_table[:, :, None] == route_table[:, None, :]
    slot_rank = jnp.sum(jnp.where(same_route & earlier[None, :, :], 1, 0), axis=2).astype(jnp.int32)
    target = route_table * capacity + slot_rank
    own_target = lax.dynamic_index_in_dim(target, group_index, 0, keepdims=False)
    placing = (jnp.arange(group_size * capacity)[:, None] == own_target[None, :]).astype(
        jnp.bfloat16
    )
    wanted = (route_table == group_index)[:, :, None] & (
        slot_rank[:, :, None] == jnp.arange(capacity)[None, None, :]
    )
    slot_hot = slot_table[:, :, None] == jnp.arange(stored)[None, None, :]
    choosing = (
        jnp.einsum("gkc,gka->gca", wanted.astype(jnp.float32), slot_hot.astype(jnp.float32))
        .reshape(group_size * capacity, stored)
        .astype(jnp.bfloat16)
    )
    store_flat = adapter_store.reshape(stored, local_width * lane_count)
    outgoing = jnp.dot(choosing, store_flat, preferred_element_type=jnp.float32).astype(
        jnp.bfloat16
    )
    chosen = outgoing.reshape(group_size * capacity, local_width, lane_count)

    def apply_adapter_update(input_rows, leading_column, trailing_column):
        sending = jnp.dot(
            placing,
            input_rows.reshape(seg_count, SEG * local_width),
            preferred_element_type=jnp.float32,
        ).astype(jnp.bfloat16)
        received = lax.all_to_all(
            sending.reshape(group_size, capacity * SEG, local_width),
            "group",
            split_axis=0,
            concat_axis=0,
            tiled=True,
        )
        received = received.reshape(group_size * capacity, SEG, local_width)
        partial_value = jnp.einsum(
            "nsd,ndr->nsr",
            received,
            chosen[:, :, leading_column : leading_column + adapter_rank_width],
            preferred_element_type=jnp.float32,
        )
        low_rank = rank_total(partial_value).astype(jnp.bfloat16)
        result = jnp.einsum(
            "nsr,ndr->nsd",
            low_rank,
            chosen[:, :, trailing_column : trailing_column + adapter_rank_width],
            preferred_element_type=jnp.float32,
        )
        returned = lax.all_to_all(
            result.reshape(group_size, capacity * SEG, local_width),
            "group",
            split_axis=0,
            concat_axis=0,
            tiled=True,
        )
        returned = returned.reshape(group_size * capacity, SEG * local_width)
        gathered = jnp.dot(
            placing.T.astype(jnp.float32),
            returned,
            precision=lax.Precision.HIGHEST,
            preferred_element_type=jnp.float32,
        )
        return gathered.reshape(row_count, local_width)

    lengths = page_counts[0] * split_count * half_size - page_trims[0]
    query_float32 = jnp.dot(
        normalized_hidden, query_matrix, preferred_element_type=jnp.float32
    ) + adapter_scale * apply_adapter_update(normalized_local, 0, 2 * adapter_rank_width)
    queries = rotate(
        query_float32.reshape(row_count, heads_dev, HD), (lengths - 1).astype(jnp.float32)
    ).astype(jnp.bfloat16)
    for level_bit in range(split_count.bit_length() - 1):
        partner = partner_2(queries, "tensor", level_bit)
        upper_bit = shard_tensor_index // 2**level_bit % 2
        queries = jnp.where(
            upper_bit == 0,
            jnp.concatenate([queries, partner], axis=1),
            jnp.concatenate([partner, queries], axis=1),
        )
    offsets = jnp.cumsum(page_counts[0]) - page_counts[0]
    page_slot = jnp.clip(
        offsets[:, None] + jnp.arange(PAGES_MAX, dtype=jnp.int32)[None, :], 0, pool_size - 1
    )
    page_ids = page_order[0][page_slot]
    cached = kv_pages[:, 0][page_ids].reshape(row_count, PAGES_MAX * half_size, 2 * HD)
    positions = (
        jnp.arange(PAGES_MAX, dtype=jnp.int32)[:, None] * (split_count * half_size)
        + part_index * half_size
        + jnp.arange(half_size, dtype=jnp.int32)[None, :]
    ).reshape(-1)
    usable = positions[None, :] < lengths[:, None]
    scores = jnp.einsum(
        "rgd,rpd->rgp", queries, cached[..., :HD], preferred_element_type=jnp.float32
    ) / math.sqrt(HD)
    masked = jnp.where(usable[:, None, :], scores, -1e30)
    row_max = jnp.max(masked, axis=2)
    weights = jnp.where(usable[:, None, :], jnp.exp(masked - row_max[..., None]), 0.0).astype(
        jnp.bfloat16
    )
    totals = jnp.sum(weights.astype(jnp.float32), axis=2)
    output_part = jnp.einsum(
        "rgp,rpd->rgd", weights, cached[..., HD:], preferred_element_type=jnp.float32
    )
    for level_bit in range(split_count.bit_length() - 1):
        other_out, other_max, other_total = partner_2(
            (output_part, row_max, totals), "tensor", level_bit
        )
        joint_max = jnp.maximum(row_max, other_max)
        own_scale = jnp.exp(row_max - joint_max)
        other_scale = jnp.exp(other_max - joint_max)
        output_part = output_part * own_scale[..., None] + other_out * other_scale[..., None]
        totals = totals * own_scale + other_total * other_scale
        row_max = joint_max
    attended_all = output_part / totals[..., None]
    attention_result = (
        lax.dynamic_slice_in_dim(attended_all, part_index * heads_dev, heads_dev, 1)
        .reshape(row_count, local_width)
        .astype(jnp.bfloat16)
    )
    partial_output = jnp.dot(attention_result, output_weight, preferred_element_type=jnp.float32)
    adapter_output = adapter_scale * apply_adapter_update(
        attention_result, adapter_rank_width, 3 * adapter_rank_width
    )
    own_cols = (
        lax.dynamic_slice_in_dim(partial_output, shard_tensor_index * local_width, local_width, 1)
        + adapter_output
    )
    partial_output = lax.dynamic_update_slice_in_dim(
        partial_output, own_cols, shard_tensor_index * local_width, 1
    )
    summed = lax.psum(partial_output, "tensor")
    layer_out = (hidden_float32 + summed).astype(jnp.bfloat16)
    return layer_out


def solution(mesh):
    in_specs = (
        P("group", None),
        P(),
        P(None, "tensor"),
        P("tensor", None),
        P("group", "tensor", None, None),
        P("group", None),
        P("group", None),
        P("group", None),
        P("group", "tensor", None),
        P(),
        P(),
    )
    out_specs = P("group", None)
    return jax.shard_map(body, mesh=mesh, in_specs=in_specs, out_specs=out_specs, check_vma=False)
```

profile of v0, /device:TPU:0, one launch (start us, length us, event | category | flops | bytes accessed | tf_op | source)
XLA Modules:
  0.0 380.9 jit_solution(1167026221294067381)
XLA Ops:
  6.5 2.2 fusion.5
  11.7 2.2 fusion.7
  20.2 4.2 %all-to-all-start = ((bf16[4,64,1024]{2,1,0:T(8,128)(2,1)}), bf16[4,64,1024]{2,1,0:T(8,128)(2,1)}, u32[]{:S(2)}, u32[]{:S(2)}) async-start(bf16[4,64,1024]{2,1,0:T(8,128)(2,1)} %reshape.285), calls=%async_computation | async-start | bytes 1048576 | tf_op jit(solution)/shard_map/all_to_all | solution.py:109
  25.3 6.8 %gather_fusion = s32[1024]{0:T(1024)S(1)} fusion(s32[192]{0:T(256)S(1)} %bitcast.51, s32[1024]{0:T(1024)S(1)} %broadcast_clamp_fusion), kind=kCustom, calls=%fused_computation | custom fusion | bytes 12288 | tf_op jit(solution)/shard_map/gather | solution.py:165
  32.4 4.6 %copy.27 = bf16[1,8,1024,256]{3,1,2,0:T(8,128)(2,1)S(1)} copy(bf16[1,8,1024,256]{3,2,1,0:T(8,128)(2,1)} %bitcast.61) | data formatting | bytes 8388608
  37.1 5.5 %convolution_convert_fusion = bf16[16,262144]{1,0:T(8,128)(2,1)} fusion(bf16[16,8]{1,0:T(8,128)(2,1)S(1)} %bitcast.65, bf16[8,262144]{1,0:T(8,128)(2,1)S(1)} %bitcast.59), kind=kOutput, calls=%fused_computation.3 | convolution fusion | flops 71303168 | bytes 12583168 | tf_op jit(solution)/shard_map/dot_general | solution.py:98
  42.7 8.5 %copy.28 = bf16[2,8,1024,256]{3,2,1,0:T(8,128)(2,1)} copy(bf16[2,8,1024,256]{3,1,2,0:T(8,128)(2,1)} %bitcast.56) | data formatting | bytes 16777216
  51.1 3.0 fusion.15
  54.2 40.2 %psum.21 = bf16[16,16,64]{2,1,0:T(8,128)(2,1)S(1)} all-reduce(f32[16,16,64]{2,1,0:T(8,128)S(1)} %fusion.15), channel_id=1, replica_groups=mesh['group'=4,'tensor'=8] {'tensor'}, use_global_device_ids=true, to_apply=%region_2.3 | all-reduce | flops 16384 | bytes 98304 | tf_op jit(solution)/shard_map/psum | solution.py:38
  94.4 4.4 %fusion.13 = f32[16,16,1024]{2,1,0:T(8,128)} fusion(bf16[16,1024,256]{2,1,0:T(8,128)(2,1)} %bitcast.53, bf16[16,16,64]{2,1,0:T(8,128)(2,1)S(1)} %psum.21), kind=kOutput, calls=%fused_computation.23 | convolution fusion | flops 33554432 | bytes 5275648 | tf_op jit(solution)/shard_map/nsr,ndr->nsd/dot_general | solution.py:124
  98.7 4.4 %all-to-all-start.1 = ((f32[4,64,1024]{2,1,0:T(8,128)}), f32[4,64,1024]{2,1,0:T(8,128)}, u32[]{:S(2)}, u32[]{:S(2)}) async-start(f32[4,64,1024]{2,1,0:T(8,128)} %bitcast.62), calls=%async_computation.1 | async-start | bytes 2097152 | tf_op jit(solution)/shard_map/all_to_all | solution.py:130
  103.2 12.4 %gather_fusion.1 = bf16[1024,32,256]{2,1,0:T(8,128)(2,1)} fusion(bf16[192,32,256]{2,1,0:T(8,128)(2,1)S(1)} %bitcast.50, s32[1024]{0:T(1024)S(1)} %broadcast_clamp_fusion.1), kind=kCustom, calls=%fused_computation.1 | custom fusion | bytes 33558528 | tf_op jit(solution)/shard_map/gather | solution.py:166
  121.4 8.1 %fusion.27 = f32[16,8,8,128]{3,1,2,0:T(8,128)S(1)} fusion(f32[128,1024]{1,0:T(8,128)S(1)} %mul.135, bf16[128,8192]{1,0:T(8,128)(2,1)S(1)} %copy-done.4, bf16[8192,1024]{1,0:T(8,128)(2,1)} %param.13), kind=kOutput, calls=%fused_computation.34 | convolution fusion | flops 2147614720 | bytes 19922944 | tf_op jit(solution)/shard_map/dot_general | solution.py:147
  129.9 5.9 %convert_reduce_fusion = (f32[128,8]{1,0:T(8,128)S(1)}, bf16[128,8,256]{2,1,0:T(8,128)(2,1)S(1)}) fusion(pred[128,256]{1,0:T(8,128)(4,1)S(1)} %broadcast_compare_fusion, bf16[128,256,256]{2,1,0:T(8,128)(2,1)} %bitcast.57, bf16[128,8,64]{2,1,0:T(8,128)(2,1)S(1)} %get-tuple-element.8, bf16[128,8,64]{2,1,0:T(8,128)(2,1)S(1)} %get-tuple-element.7), kind=kOutput, calls=%fused_computation.36 | convolution fusion | flops 69468416 | bytes 9506816 | tf_op jit(solution)/shard_map/sub | solution.py:178
  135.8 4.6 %fusion.31 = bf16[128,8,128]{2,1,0:T(8,128)(2,1)S(1)} fusion(bf16[128,8,256]{2,1,0:T(8,128)(2,1)S(1)} %get-tuple-element.13, bf16[128,256,256]{2,1,0:T(8,128)(2,1)} %bitcast.58, f32[128,8]{1,0:T(8,128)S(1)} %get-tuple-element.12), kind=kOutput, calls=%fused_computation.38 | convolution fusion | flops 67371008 | bytes 9179136 | tf_op jit(solution)/shard_map/rgp,rpd->rgd/dot_general | solution.py:182
  141.0 11.2 %all_to_all.20 = bf16[4,64,1024]{2,1,0:T(8,128)(2,1)S(1)} all-to-all(bf16[4,64,1024]{2,1,0:T(8,128)(2,1)S(1)} %reshape.295), channel_id=1, replica_groups=mesh['group'=4,'tensor'=8] {'group'}, dimensions={0} | all-to-all | bytes 1048576 | tf_op jit(solution)/shard_map/all_to_all | solution.py:109
  152.2 3.5 fusion.11
  155.7 34.2 %psum.22 = bf16[16,16,64]{2,1,0:T(8,128)(2,1)S(1)} all-reduce(f32[16,16,64]{2,1,0:T(8,128)S(1)} %fusion.11), channel_id=1, replica_groups=mesh['group'=4,'tensor'=8] {'tensor'}, use_global_device_ids=true, to_apply=%region_6.7 | all-reduce | flops 16384 | bytes 98304 | tf_op jit(solution)/shard_map/psum | solution.py:38
  189.9 4.5 %fusion.9 = f32[16,16,1024]{2,1,0:T(8,128)} fusion(bf16[16,1024,256]{2,1,0:T(8,128)(2,1)} %bitcast.55, bf16[16,16,64]{2,1,0:T(8,128)(2,1)S(1)} %psum.22), kind=kOutput, calls=%fused_computation.19 | convolution fusion | flops 33554432 | bytes 5275648 | tf_op jit(solution)/shard_map/nsr,ndr->nsd/dot_general | solution.py:124
  194.3 3.5 all-to-all-start.3
  198.1 10.1 %fusion.34 = f32[128,8192]{1,0:T(8,128)} fusion(bf16[1024,8192]{1,0:T(8,128)(2,1)} %param.14, bf16[16,8,8,128]{3,2,1,0:T(8,128)(2,1)S(1)} %bitcast.64), kind=kOutput, calls=%fused_computation.42 | convolution fusion | flops 2147483648 | bytes 21233664 | tf_op jit(solution)/shard_map/dot_general | solution.py:201
  208.2 4.0 %all-to-all-done.3 = f32[4,64,1024]{2,1,0:T(8,128)S(1)} async-done(((f32[4,64,1024]{2,1,0:T(8,128)}), f32[4,64,1024]{2,1,0:T(8,128)S(1)}, u32[]{:S(2)}, u32[]{:S(2)}) %all-to-all-start.3) | async-done | bytes 1048608 | tf_op jit(solution)/shard_map/all_to_all | solution.py:130
  215.0 154.5 %all-reduce.2.cloned.1.call-done = f32[128,8192]{1,0:T(8,128)} async-done(((f32[128,8192]{1,0:T(8,128)}), f32[128,8192]{1,0:T(8,128)}) %all-reduce.2.cloned.1.call-update) | async-done | bytes 4194320 | tf_op jit(solution)/shard_map/psum | solution.py:212
  369.5 4.6 %fusion.8 = bf16[128,8192]{1,0:T(8,128)(2,1)} fusion(f32[128,8192]{1,0:T(8,128)} %all-reduce.2.cloned.1.call-done, bf16[128,8192]{1,0:T(8,128)(2,1)} %param.11), kind=kLoop, calls=%fused_computation.18 | loop fusion | flops 3145728 | bytes 8388608 | tf_op jit(solution)/shard_map/convert_element_type | solution.py:213
  (65 shorter events, 20.1 us)
Async XLA Ops:
  6.5 96.6 %copy-start = (bf16[192,1,32,256]{3,2,1,0:T(8,128)(2,1)S(1)}, bf16[192,1,32,256]{3,2,1,0:T(8,128)(2,1)}, u32[]{:S(2)}) copy-start(bf16[192,1,32,256]{3,2,1,0:T(8,128)(2,1)} %param.15) | copy-start | bytes 9437188
  8.8 15.7 %copy-start.6 = (s32[32]{0:T(128)S(1)}, s32[32]{0:T(128)}, u32[]{:S(2)}) copy-start(s32[32]{0:T(128)} %param.21) | copy-start | bytes 388
  8.8 15.9 %copy-start.5 = (s32[1,128]{1,0:T(1,128)S(1)}, s32[1,128]{1,0:T(1,128)}, u32[]{:S(2)}) copy-start(s32[1,128]{1,0:T(1,128)} %param.17) | copy-start | bytes 1540
  11.7 13.4 %copy-start.7 = (s32[1,128]{1,0:T(1,128)S(1)}, s32[1,128]{1,0:T(1,128)}, u32[]{:S(2)}) copy-start(s32[1,128]{1,0:T(1,128)} %param.18) | copy-start | bytes 1540
  11.7 13.6 %copy-start.2 = (s32[1,192]{1,0:T(1,128)S(1)}, s32[1,192]{1,0:T(1,128)}, u32[]{:S(2)}) copy-start(s32[1,192]{1,0:T(1,128)} %param.16) | copy-start | bytes 2308
  13.9 1.3 copy-start.3
  20.2 30.9 %all-to-all-start = ((bf16[4,64,1024]{2,1,0:T(8,128)(2,1)}), bf16[4,64,1024]{2,1,0:T(8,128)(2,1)}, u32[]{:S(2)}, u32[]{:S(2)}) async-start(bf16[4,64,1024]{2,1,0:T(8,128)(2,1)} %reshape.285), calls=%async_computation | async-start | bytes 1048576 | tf_op jit(solution)/shard_map/all_to_all | solution.py:109
  98.7 18.7 %all-to-all-start.1 = ((f32[4,64,1024]{2,1,0:T(8,128)}), f32[4,64,1024]{2,1,0:T(8,128)}, u32[]{:S(2)}, u32[]{:S(2)}) async-start(f32[4,64,1024]{2,1,0:T(8,128)} %bitcast.62), calls=%async_computation.1 | async-start | bytes 2097152 | tf_op jit(solution)/shard_map/all_to_all | solution.py:130
  115.6 5.8 %copy-start.4 = (bf16[128,8192]{1,0:T(8,128)(2,1)S(1)}, bf16[128,8192]{1,0:T(8,128)(2,1)}, u32[]{:S(2)}) copy-start(bf16[128,8192]{1,0:T(8,128)(2,1)} %copy-done.3) | copy-start | bytes 6291460
  194.3 17.9 %all-to-all-start.3 = ((f32[4,64,1024]{2,1,0:T(8,128)}), f32[4,64,1024]{2,1,0:T(8,128)S(1)}, u32[]{:S(2)}, u32[]{:S(2)}) async-start(f32[4,64,1024]{2,1,0:T(8,128)} %bitcast.11), calls=%async_computation.3 | async-start | bytes 2097152 | tf_op jit(solution)/shard_map/all_to_all | solution.py:130
  197.9 171.6 %all-reduce.2.cloned.1.call-start = ((), (), s32[]{:S(2)}) async-start(), calls=%async_computation.4 | async-start | bytes 8388608 | tf_op jit(solution)/shard_map/psum | solution.py:212
  215.0 159.1 %copy-start.1 = (bf16[192,1,32,256]{3,2,1,0:T(8,128)(2,1)S(1)}, bf16[192,1,32,256]{3,2,1,0:T(8,128)(2,1)}, u32[]{:S(2)}) copy-start(bf16[192,1,32,256]{3,2,1,0:T(8,128)(2,1)} %param.15) | copy-start | bytes 9437188
Sparse Core Ops, SparseCore 0:
  215.1 154.3 all-reduce.1
where the time goes:
time: 382 us; the launch traced here: 381 us
  waiting for transfers between devices  160 us (42%)
  blocking collectives  85.6 us (22%)
  matrix products  53.8 us (14%)
  local copies, waits for them, and re-layouts  41.1 us (11%)
  other arithmetic  14.4 us (4%)
  between operations  13.7 us (4%)
  starting transfers between devices  12.4 us (3%)
    psum x1, waiting for transfers between devices, body(): summed = lax.psum(partial_output, 'tensor')  154 us
    psum x2, blocking collectives, rank_total(): return lax.psum(partial_value, 'tensor')  74.4 us
    unnamed x20, local copies, waits for them, and re-layouts  15 us
    gather x1, local copies, waits for them, and re-layouts, body(): kv_pages[:, 0][page_ids].reshape(row_count, PAGES_MAX * half_size, 2 * HD)  12.4 us
    all_to_all x1, blocking collectives, apply_adapter_update(): lax.all_to_all(sending.reshape(group_size, capacity * SEG, local_width),...  11.2 us
    dot_general x1, matrix products, body(): jnp.dot(attention_result, output_weight, preferred_element_type=jnp.float32)  10.1 us
    dot_general x2, matrix products, apply_adapter_update(): jnp.einsum('nsr,ndr->nsd', low_rank, chosen[:, :, trailing_column:trailin...  8.83 us
    dot_general x1, matrix products, body(): jnp.dot(normalized_hidden, query_matrix, preferred_element_type=jnp.float32)  8.1 us
  transfers between devices with their start and end apart: 4, of which 3 were waited for; matrix products, arithmetic and copies ran while one was open for 13% of the time, Pallas kernels for 0%

commit v1 on v0

--- a/solution.py
+++ b/solution.py
@@ -209,7 +209,9 @@
     partial_output = lax.dynamic_update_slice_in_dim(
         partial_output, own_cols, shard_tensor_index * local_width, 1
     )
-    summed = lax.psum(partial_output, "tensor")
+    summed = partial_output
+    for hop in (1, 2, 4):
+        summed = summed + lax.ppermute(summed, "tensor", [(dev, dev ^ hop) for dev in range(8)])
     layer_out = (hidden_float32 + summed).astype(jnp.bfloat16)
     return layer_out
 

time: 382 us -> 579 us (1.52)
  waiting for transfers between devices: 160 us -> 370 us
  between operations: 13.7 us -> 0.33 us
    ppermute x0 -> x3, waiting for transfers between devices: none -> 364 us  [body(): lax.ppermute(summed, 'tensor', [(dev, dev ^ hop) for dev in range(8)])]
    psum x1 -> x0, waiting for transfers between devices: 154 us -> none  [body(): summed = lax.psum(partial_output, 'tensor')]
    unnamed x20 -> x22, local copies, waits for them, and re-layouts: 15 us -> 15 us
  transfers between devices with their start and end apart: 4 -> 6, of which waited for: 3 -> 5; matrix products, arithmetic and copies ran while one was open for 13% -> 9% of each run, Pallas kernels for 0% -> 0%
where the time goes in v1:
time: 579 us; the launch traced here: 578 us
  waiting for transfers between devices  370 us (64%)
  blocking collectives  85.6 us (15%)
  matrix products  53.8 us (9%)
  local copies, waits for them, and re-layouts  41.1 us (7%)
  other arithmetic  15 us (3%)
  starting transfers between devices  12.7 us (2%)
    ppermute x3, waiting for transfers between devices, body(): lax.ppermute(summed, 'tensor', [(dev, dev ^ hop) for dev in range(8)])  364 us
    psum x2, blocking collectives, rank_total(): return lax.psum(partial_value, 'tensor')  74.4 us
    unnamed x22, local copies, waits for them, and re-layouts  15 us
    gather x1, local copies, waits for them, and re-layouts, body(): kv_pages[:, 0][page_ids].reshape(row_count, PAGES_MAX * half_size, 2 * HD)  12.4 us
  transfers between devices with their start and end apart: 6, of which 5 were waited for; matrix products, arithmetic and copies ran while one was open for 9% of the time, Pallas kernels for 0%

profile of v1, /device:TPU:0, one launch (start us, length us, event | category | flops | bytes accessed | tf_op | source)
XLA Modules:
  0.0 578.3 jit_solution(12545940444229090303)
XLA Ops:
  13.7 4.2 all-to-all-start
  18.8 6.8 %gather_fusion = s32[1024]{0:T(1024)S(1)} fusion(s32[192]{0:T(256)S(1)} %bitcast.51, s32[1024]{0:T(1024)S(1)} %broadcast_clamp_fusion), kind=kCustom, calls=%fused_computation | custom fusion | bytes 12288 | tf_op jit(solution)/shard_map/gather | solution.py:165
  25.8 4.6 copy.27
  30.6 5.5 convolution_convert_fusion
  36.1 8.5 %copy.28 = bf16[2,8,1024,256]{3,2,1,0:T(8,128)(2,1)} copy(bf16[2,8,1024,256]{3,1,2,0:T(8,128)(2,1)} %bitcast.56) | data formatting | bytes 16777216
  44.6 3.0 fusion.15
  47.6 40.2 %psum.14 = bf16[16,16,64]{2,1,0:T(8,128)(2,1)S(1)} all-reduce(f32[16,16,64]{2,1,0:T(8,128)S(1)} %fusion.15), channel_id=1, replica_groups=mesh['group'=4,'tensor'=8] {'tensor'}, use_global_device_ids=true, to_apply=%region_2.3 | all-reduce | flops 16384 | bytes 98304 | tf_op jit(solution)/shard_map/psum | solution.py:38
  87.8 4.4 fusion.13
  92.2 4.4 all-to-all-start.1
  96.7 12.4 %gather_fusion.1 = bf16[1024,32,256]{2,1,0:T(8,128)(2,1)} fusion(bf16[192,32,256]{2,1,0:T(8,128)(2,1)S(1)} %bitcast.50, s32[1024]{0:T(1024)S(1)} %broadcast_clamp_fusion.1), kind=kCustom, calls=%fused_computation.1 | custom fusion | bytes 33558528 | tf_op jit(solution)/shard_map/gather | solution.py:166
  114.9 8.1 %fusion.27 = f32[16,8,8,128]{3,1,2,0:T(8,128)S(1)} fusion(f32[128,1024]{1,0:T(8,128)S(1)} %mul.135, bf16[128,8192]{1,0:T(8,128)(2,1)S(1)} %copy-done.5, bf16[8192,1024]{1,0:T(8,128)(2,1)} %param.13), kind=kOutput, calls=%fused_computation.34 | convolution fusion | flops 2147614720 | bytes 19922944 | tf_op jit(solution)/shard_map/dot_general | solution.py:147
  123.4 5.9 %convert_reduce_fusion = (f32[128,8]{1,0:T(8,128)S(1)}, bf16[128,8,256]{2,1,0:T(8,128)(2,1)S(1)}) fusion(pred[128,256]{1,0:T(8,128)(4,1)S(1)} %broadcast_compare_fusion, bf16[128,256,256]{2,1,0:T(8,128)(2,1)} %bitcast.57, bf16[128,8,64]{2,1,0:T(8,128)(2,1)S(1)} %get-tuple-element.8, bf16[128,8,64]{2,1,0:T(8,128)(2,1)S(1)} %get-tuple-element.7), kind=kOutput, calls=%fused_computation.36 | convolution fusion | flops 69468416 | bytes 9506816 | tf_op jit(solution)/shard_map/sub | solution.py:178
  129.2 4.6 fusion.31
  134.5 11.2 %all_to_all.20 = bf16[4,64,1024]{2,1,0:T(8,128)(2,1)S(1)} all-to-all(bf16[4,64,1024]{2,1,0:T(8,128)(2,1)S(1)} %reshape.295), channel_id=1, replica_groups=mesh['group'=4,'tensor'=8] {'group'}, dimensions={0} | all-to-all | bytes 1048576 | tf_op jit(solution)/shard_map/all_to_all | solution.py:109
  145.7 3.5 fusion.11
  149.2 34.2 %psum.15 = bf16[16,16,64]{2,1,0:T(8,128)(2,1)S(1)} all-reduce(f32[16,16,64]{2,1,0:T(8,128)S(1)} %fusion.11), channel_id=1, replica_groups=mesh['group'=4,'tensor'=8] {'tensor'}, use_global_device_ids=true, to_apply=%region_6.7 | all-reduce | flops 16384 | bytes 98304 | tf_op jit(solution)/shard_map/psum | solution.py:38
  183.4 4.5 fusion.9
  187.8 3.7 all-to-all-start.3
  191.6 10.1 %fusion.34 = f32[128,8192]{1,0:T(8,128)} fusion(bf16[1024,8192]{1,0:T(8,128)(2,1)} %param.14, bf16[16,8,8,128]{3,2,1,0:T(8,128)(2,1)S(1)} %bitcast.64), kind=kOutput, calls=%fused_computation.42 | convolution fusion | flops 2147483648 | bytes 21233664 | tf_op jit(solution)/shard_map/dot_general | solution.py:201
  201.6 4.1 all-to-all-done.3
  208.5 92.2 %collective-permute-done = f32[128,8192]{1,0:T(8,128)S(1)} collective-permute-done((f32[128,8192]{1,0:T(8,128)}, f32[128,8192]{1,0:T(8,128)S(1)}, u32[]{:S(2)}, u32[]{:S(2)}) %collective-permute-start) | collective-permute-done | bytes 4194336 | tf_op jit(solution)/shard_map/ppermute | solution.py:214
  300.7 2.7 add.137
  303.5 91.1 %collective-permute-done.1 = f32[128,8192]{1,0:T(8,128)S(1)} collective-permute-done((f32[128,8192]{1,0:T(8,128)S(1)}, f32[128,8192]{1,0:T(8,128)S(1)}, u32[]{:S(2)}, u32[]{:S(2)}) %collective-permute-start.1) | collective-permute-done | bytes 4194336 | tf_op jit(solution)/shard_map/ppermute | solution.py:214
  395.4 181.0 %collective-permute-done.2 = f32[128,8192]{1,0:T(8,128)S(1)} collective-permute-done((f32[128,8192]{1,0:T(8,128)S(1)}, f32[128,8192]{1,0:T(8,128)S(1)}, u32[]{:S(2)}, u32[]{:S(2)}) %collective-permute-start.2) | collective-permute-done | bytes 4194336 | tf_op jit(solution)/shard_map/ppermute | solution.py:214
  (72 shorter events, 27.0 us)
Async XLA Ops:
  0.0 96.6 %copy-start = (bf16[192,1,32,256]{3,2,1,0:T(8,128)(2,1)S(1)}, bf16[192,1,32,256]{3,2,1,0:T(8,128)(2,1)}, u32[]{:S(2)}) copy-start(bf16[192,1,32,256]{3,2,1,0:T(8,128)(2,1)} %param.15) | copy-start | bytes 9437188
  2.2 15.7 %copy-start.7 = (s32[32]{0:T(128)S(1)}, s32[32]{0:T(128)}, u32[]{:S(2)}) copy-start(s32[32]{0:T(128)} %param.21) | copy-start | bytes 388
  2.2 15.9 %copy-start.6 = (s32[1,128]{1,0:T(1,128)S(1)}, s32[1,128]{1,0:T(1,128)}, u32[]{:S(2)}) copy-start(s32[1,128]{1,0:T(1,128)} %param.17) | copy-start | bytes 1540
  5.1 13.4 %copy-start.8 = (s32[1,128]{1,0:T(1,128)S(1)}, s32[1,128]{1,0:T(1,128)}, u32[]{:S(2)}) copy-start(s32[1,128]{1,0:T(1,128)} %param.18) | copy-start | bytes 1540
  5.1 13.7 %copy-start.2 = (s32[1,192]{1,0:T(1,128)S(1)}, s32[1,192]{1,0:T(1,128)}, u32[]{:S(2)}) copy-start(s32[1,192]{1,0:T(1,128)} %param.16) | copy-start | bytes 2308
  7.3 1.3 copy-start.4
  13.7 30.9 %all-to-all-start = ((bf16[4,64,1024]{2,1,0:T(8,128)(2,1)}), bf16[4,64,1024]{2,1,0:T(8,128)(2,1)}, u32[]{:S(2)}, u32[]{:S(2)}) async-start(bf16[4,64,1024]{2,1,0:T(8,128)(2,1)} %reshape.285), calls=%async_computation | async-start | bytes 1048576 | tf_op jit(solution)/shard_map/all_to_all | solution.py:109
  92.2 18.7 %all-to-all-start.1 = ((f32[4,64,1024]{2,1,0:T(8,128)}), f32[4,64,1024]{2,1,0:T(8,128)}, u32[]{:S(2)}, u32[]{:S(2)}) async-start(f32[4,64,1024]{2,1,0:T(8,128)} %bitcast.62), calls=%async_computation.1 | async-start | bytes 2097152 | tf_op jit(solution)/shard_map/all_to_all | solution.py:130
  109.1 5.8 copy-start.5
  187.8 17.9 %all-to-all-start.3 = ((f32[4,64,1024]{2,1,0:T(8,128)}), f32[4,64,1024]{2,1,0:T(8,128)S(1)}, u32[]{:S(2)}, u32[]{:S(2)}) async-start(f32[4,64,1024]{2,1,0:T(8,128)} %bitcast.11), calls=%async_computation.3 | async-start | bytes 2097152 | tf_op jit(solution)/shard_map/all_to_all | solution.py:130
  208.4 92.2 %collective-permute-start = (f32[128,8192]{1,0:T(8,128)}, f32[128,8192]{1,0:T(8,128)S(1)}, u32[]{:S(2)}, u32[]{:S(2)}) collective-permute-start(f32[128,8192]{1,0:T(8,128)} %add_dynamic-update-slice_fusion), channel_id=1, source_target_pairs={{0,1},{1,0},{2,3},{3,2},{4,5},{5,4},{6,7},{7,6},{8,9},{9,8},{10,11... | collective-permute-start | bytes 12582920 | tf_op jit(solution)/shard_map/ppermute | solution.py:214
  303.4 272.9 %copy-start.3 = (bf16[128,8192]{1,0:T(8,128)(2,1)S(1)}, bf16[128,8192]{1,0:T(8,128)(2,1)}, u32[]{:S(2)}) copy-start(bf16[128,8192]{1,0:T(8,128)(2,1)} %param.11) | copy-start | bytes 6291460
  303.4 91.2 %collective-permute-start.1 = (f32[128,8192]{1,0:T(8,128)S(1)}, f32[128,8192]{1,0:T(8,128)S(1)}, u32[]{:S(2)}, u32[]{:S(2)}) collective-permute-start(f32[128,8192]{1,0:T(8,128)S(1)} %add.137), channel_id=1, source_target_pairs={{0,2},{1,3},{2,0},{3,1},{4,6},{5,7},{6,4},{7,5},{8,10},{9,11},{10,... | collective-permute-start | bytes 12582920 | tf_op jit(solution)/shard_map/ppermute | solution.py:214
  394.6 183.7 %copy-start.1 = (bf16[192,1,32,256]{3,2,1,0:T(8,128)(2,1)S(1)}, bf16[192,1,32,256]{3,2,1,0:T(8,128)(2,1)}, u32[]{:S(2)}) copy-start(bf16[192,1,32,256]{3,2,1,0:T(8,128)(2,1)} %param.15) | copy-start | bytes 9437188
  395.2 181.2 %collective-permute-start.2 = (f32[128,8192]{1,0:T(8,128)S(1)}, f32[128,8192]{1,0:T(8,128)S(1)}, u32[]{:S(2)}, u32[]{:S(2)}) collective-permute-start(f32[128,8192]{1,0:T(8,128)S(1)} %add.138), channel_id=1, source_target_pairs={{0,4},{1,5},{2,6},{3,7},{4,0},{5,1},{6,2},{7,3},{8,12},{9,13},{10,... | collective-permute-start | bytes 12582920 | tf_op jit(solution)/shard_map/ppermute | solution.py:214
